TPU v7x, 32 devices: a whole 2x2x4 slice. The times are simulated.
32 devices in a mesh: wide: 8 (over z, y), narrow: 4 (over x, core).
Axes of the slice: x: 2, y: 2, z: 4, core: 2. Of those that a mesh axis runs over, the one named last changes fastest.
Arguments:
- frames: bfloat16 [256, 2, 256, 256], P(('wide', 'narrow')), may hold values from -120 to 120
- sketch: bfloat16 [256, 128], replicated, may hold values from -0.3 to 2.3
- kernel_taps: bfloat16 [64], replicated, may hold values from -0.3 to 1.1
Outputs:
- basis: float32 [128, 32768], P(None, ('wide', 'narrow'))
- factor: float32 [128, 128], replicated
All inputs are finite; a program needn't handle non-finite values.
Results may differ from a plain program's by a relative error of at most 0.0043.
Values may be sent and summed in bfloat16 or wider, within the bound.
No kernel may reach another device: no remote copies, remote signals or barrier semaphores. Data moves between devices by JAX's collectives and lax.ppermute only.
A program may use at most 64 MiB of HBM per device.

v0:
```python
import jax
import jax.numpy as jnp
from jax import lax
from jax.sharding import PartitionSpec as P


def gauss_taps(spread):
    position = jnp.arange(15, dtype=jnp.float32) - 7.0
    weights = jnp.exp(-position * position / (2.0 * spread * spread))
    return weights / jnp.sum(weights)


def band_matrix(spread, length):
    outputs = length // 2
    offset_index = (
        jnp.arange(length, dtype=jnp.int32)[None, :]
        - 2 * jnp.arange(outputs, dtype=jnp.int32)[:, None]
        + 7
    )
    weights = gauss_taps(spread)
    matrix = jnp.zeros((outputs, length), jnp.float32)
    for offset in range(15):
        matrix = matrix + jnp.where(offset_index == offset, weights[offset], jnp.float32(0.0))
    return matrix


def filter_volumes(frames_block):
    volume = frames_block.astype(jnp.float32)
    row_count = volume.shape[-2]
    col_count = volume.shape[-1]
    half = col_count // 2
    column_bands = jnp.concatenate(
        [band_matrix(1.5, col_count), band_matrix(3.0, col_count)], axis=0
    )
    column_pass = jnp.einsum(
        "...rc,oc->...ro", volume, column_bands, precision=lax.Precision.HIGHEST
    )
    narrow_pass = jnp.einsum(
        "or,...rc->...oc",
        band_matrix(1.5, row_count),
        column_pass[..., :half],
        precision=lax.Precision.HIGHEST,
    )
    broad_pass = jnp.einsum(
        "or,...rc->...oc",
        band_matrix(3.0, row_count),
        column_pass[..., half:],
        precision=lax.Precision.HIGHEST,
    )
    return (narrow_pass - broad_pass).astype(jnp.bfloat16)


def build_toeplitz(kernel_taps, length):
    lag_index = (
        jnp.arange(length, dtype=jnp.int32)[:, None] - jnp.arange(length, dtype=jnp.int32)[None, :]
    )
    toeplitz = jnp.zeros((length, length), jnp.float32)
    for offset in range(kernel_taps.shape[0]):
        toeplitz = toeplitz + jnp.where(
            lag_index == offset, kernel_taps[offset].astype(jnp.float32), jnp.float32(0.0)
        )
    return toeplitz.astype(jnp.bfloat16)


def high_dot(left, right):
    return jnp.dot(left, right, precision=lax.Precision.HIGHEST, preferred_element_type=jnp.float32)


def shards(frames, sketch, kernel_taps):
    filtered = filter_volumes(frames)
    per_device = frames.shape[0]
    flattened = filtered.reshape(per_device, -1)
    voxel_count = flattened.shape[1]
    group_size = lax.axis_size(("wide", "narrow"))
    block = voxel_count // group_size
    length = per_device * group_size
    toeplitz = build_toeplitz(kernel_taps, length)
    arranged = flattened.reshape(1, per_device, group_size, block)
    received = lax.all_to_all(arranged, ("wide", "narrow"), split_axis=2, concat_axis=0, tiled=True)
    deconvolved = jnp.dot(
        toeplitz, received.reshape(length, received.shape[3]), preferred_element_type=jnp.float32
    ).astype(jnp.bfloat16)
    sketched = lax.dot_general(
        sketch, deconvolved, (((0,), (0,)), ((), ())), preferred_element_type=jnp.float32
    )
    deconvolved, sketched = (deconvolved, sketched)
    series = deconvolved.astype(jnp.float32)
    local_gram = (
        lax.dot_general(
            deconvolved, deconvolved, (((1,), (1,)), ((), ())), preferred_element_type=jnp.float32
        )
        / voxel_count
    )
    data_gram = lax.psum(local_gram, ("wide", "narrow"))
    sketch_full = sketch.astype(jnp.float32)
    weighted = high_dot(data_gram, sketch_full)
    first_lower = jnp.linalg.cholesky(high_dot(sketch_full.T, weighted))
    projected = jax.scipy.linalg.solve_triangular(first_lower, weighted.T, lower=True).T
    second_lower = jnp.linalg.cholesky(high_dot(projected.T, high_dot(data_gram, projected)))
    combined = jax.scipy.linalg.solve_triangular(second_lower, projected.T, lower=True)
    basis = high_dot(combined, series)
    factor = second_lower.T
    return (basis, factor)


def solution(mesh):
    return jax.shard_map(
        shards,
        mesh=mesh,
        in_specs=(P(("wide", "narrow"), None, None, None), P(), P()),
        out_specs=(P(None, ("wide", "narrow")), P()),
        check_vma=False,
    )
```

profile of v0, /device:TPU:0, one launch (start us, length us, event | category | flops | bytes accessed | tf_op | source)
XLA Modules:
  0.0 296.3 jit_solution(4108505157623894362)
XLA Ops:
  7.2 0.0 copy-start
  7.2 0.6 fusion.237
  7.8 0.6 fusion.238
  8.4 0.7 broadcast_divide_fusion.1
  9.1 0.7 fusion.341
  9.8 0.7 broadcast_divide_fusion
  10.4 0.7 fusion.342
  11.1 9.6 %select_add_fusion.1 = f32[128,256]{1,0:T(8,128)S(1)} fusion(f32[]{:T(128)} %bitcast.78, f32[]{:T(128)} %bitcast.77, f32[]{:T(128)} %bitcast.76, f32[]{:T(128)} %bitcast.75, f32[]{:T(128)} %bitcast.74, f32[]{:T(128)} %bitcast.73, f32[]{:T(128)} %bitcast.72, f32[]{:T(128)} %bitcast.71, f32[]{:T(128)} %bitcast.70, f32[]{:T(128)} %bitcast.69, f32[]{:T(128)} %bitcast.68, ...), kind=kLoop, calls=%fused_computation.85 | loop fusion | flops 1507328 | bytes 131644 | tf_op jit(solution)/shard_map/add | solution.py:23
  20.7 9.7 %select_add_fusion = f32[128,256]{1,0:T(8,128)S(1)} fusion(f32[]{:T(128)} %bitcast.93, f32[]{:T(128)} %bitcast.92, f32[]{:T(128)} %bitcast.91, f32[]{:T(128)} %bitcast.90, f32[]{:T(128)} %bitcast.89, f32[]{:T(128)} %bitcast.88, f32[]{:T(128)} %bitcast.87, f32[]{:T(128)} %bitcast.86, f32[]{:T(128)} %bitcast.85, f32[]{:T(128)} %bitcast.84, f32[]{:T(128)} %bitcast.83, ...), kind=kLoop, calls=%fused_computation.84 | loop fusion | flops 1507328 | bytes 131644 | tf_op jit(solution)/shard_map/add | solution.py:23
  30.4 1.9 convolution_bitcast_fusion
  32.3 11.5 %fusion = f32[8,2,128,128]{3,2,1,0:T(8,128)S(1)} fusion(f32[8,2,256,256]{2,3,1,0:T(8,128)S(1)} %convolution_bitcast_fusion, f32[]{:T(128)} %bitcast.93, f32[]{:T(128)} %bitcast.92, f32[]{:T(128)} %bitcast.91, f32[]{:T(128)} %bitcast.90, f32[]{:T(128)} %bitcast.89, f32[]{:T(128)} %bitcast.88, f32[]{:T(128)} %bitcast.87, f32[]{:T(128)} %bitcast.86, ...), kind=kOutput, calls=%fused_computation.1 | convolution fusion | flops 806813696 | bytes 3146300 | tf_op jit(solution)/shard_map/or,...rc->...oc/dot_general | solution.py:44
  43.8 11.4 %fusion.10 = bf16[8,2,128,128]{2,3,1,0:T(8,128)(2,1)S(1)} fusion(f32[8,2,128,128]{3,2,1,0:T(8,128)S(1)} %fusion, f32[8,2,256,256]{2,3,1,0:T(8,128)S(1)} %convolution_bitcast_fusion, f32[]{:T(128)} %bitcast.78, f32[]{:T(128)} %bitcast.77, f32[]{:T(128)} %bitcast.76, f32[]{:T(128)} %bitcast.75, f32[]{:T(128)} %bitcast.74, f32[]{:T(128)} %bitcast.73, ...), kind=kOutput, calls=%fused_computation.8 | convolution fusion | flops 807337984 | bytes 3670588 | tf_op jit(solution)/shard_map/or,...rc->...oc/dot_general | solution.py:38
  55.2 0.0 copy-start.1
  55.2 0.3 copy.13
  55.5 0.2 reshape_reshape.3
  55.7 1.1 copy.14
  56.8 7.3 %all-to-all-start = ((bf16[1,8,32,1024]{3,1,0,2:T(8,128)(2,1)}), bf16[1,8,32,1024]{3,1,0,2:T(8,128)(2,1)S(1)}, u32[]{:S(2)}, u32[]{:S(2)}) async-start(bf16[1,8,32,1024]{3,1,0,2:T(8,128)(2,1)} %copy.14), calls=%async_computation | async-start | bytes 1048576 | tf_op jit(solution)/shard_map/all_to_all | solution.py:79
  64.2 0.2 all-reduce.2.cloned.1.call-start
  64.4 0.0 copy-done.1
  64.4 0.7 fusion.338
  70.2 0.7 fusion.337
  83.5 0.7 fusion.339
  102.4 0.7 fusion.340
  107.5 0.0 copy-start.2
  107.5 0.0 all-to-all-done
  107.5 1.1 convolution_convert_fusion
  108.6 1.0 convolution_multiply_fusion
  109.6 0.0 all-reduce.2.cloned.1.call-update
  109.7 128.0 %all-reduce.2.cloned.1.call-done = f32[256,256]{1,0:T(8,128)} async-done(((f32[256,256]{1,0:T(8,128)}), f32[256,256]{1,0:T(8,128)}) %all-reduce.2.cloned.1.call-update) | async-done | bytes 262160 | tf_op jit(solution)/shard_map/psum | solution.py:94
  237.7 0.0 copy-done.2
  237.7 1.2 fusion.343
  238.9 0.3 fusion.344
  239.2 0.1 copy.15
  239.3 11.7 %cholesky.44 = f32[128,128]{1,0:T(8,128)S(1)} custom-call(f32[128,128]{1,0:T(8,128)S(1)} %add_multiply_fusion), custom_call_target="Cholesky" | custom-call | tf_op jit(solution)/shard_map/jit(cholesky)/cholesky | solution.py:97
  251.1 0.6 compare_reduce_fusion.1
  251.7 0.7 fusion.228
  252.4 9.8 %custom-call.6 = f32[1,128,128]{1,2,0:T(8,128)S(1)} custom-call(f32[1,128,128]{2,1,0:T(8,128)S(1)} %fusion.228), custom_call_target="InvertDiagBlocksLowerTriangular" | custom-call | tf_op jit(solution)/shard_map/jit(_solve_triangular)/triangular_solve | solution.py:98
  262.2 0.3 fusion.82
  262.5 1.3 fusion.345
  263.8 0.3 fusion.346
  264.1 0.1 copy.16
  264.2 11.9 %cholesky.55 = f32[128,128]{1,0:T(8,128)S(1)} custom-call(f32[128,128]{1,0:T(8,128)S(1)} %fusion.231), custom_call_target="Cholesky" | custom-call | tf_op jit(solution)/shard_map/jit(cholesky)/cholesky | solution.py:99
  276.1 0.6 compare_reduce_fusion
  276.8 0.7 fusion.236
  277.4 9.8 %custom-call.7 = f32[1,128,128]{1,2,0:T(8,128)S(1)} custom-call(f32[1,128,128]{2,1,0:T(8,128)S(1)} %get-tuple-element.11), custom_call_target="InvertDiagBlocksLowerTriangular" | custom-call | tf_op jit(solution)/shard_map/jit(_solve_triangular)/triangular_solve | solution.py:100
  287.3 0.3 fusion.229
  287.6 1.2 fusion.347
  288.7 0.7 copy.17
  (6 shorter events, 0.1 us)
Async XLA Ops:
  7.2 23.2 %copy-start = (bf16[8,2,256,256]{3,2,1,0:T(8,128)(2,1)S(1)}, bf16[8,2,256,256]{3,2,1,0:T(8,128)(2,1)}, u32[]{:S(2)}) copy-start(bf16[8,2,256,256]{3,2,1,0:T(8,128)(2,1)} %param.6) | copy-start | bytes 6291460
  55.2 9.2 %copy-start.1 = (bf16[64]{0:T(256)(128)(2,1)S(1)}, bf16[64]{0:T(256)(128)(2,1)}, u32[]{:S(2)}) copy-start(bf16[64]{0:T(256)(128)(2,1)} %param.8) | copy-start | bytes 388
  56.8 50.7 %all-to-all-start = ((bf16[1,8,32,1024]{3,1,0,2:T(8,128)(2,1)}), bf16[1,8,32,1024]{3,1,0,2:T(8,128)(2,1)S(1)}, u32[]{:S(2)}, u32[]{:S(2)}) async-start(bf16[1,8,32,1024]{3,1,0,2:T(8,128)(2,1)} %copy.14), calls=%async_computation | async-start | bytes 1048576 | tf_op jit(solution)/shard_map/all_to_all | solution.py:79
  64.2 173.5 %all-reduce.2.cloned.1.call-start = ((), (), s32[]{:S(2)}) async-start(), calls=%async_computation.1 | async-start | bytes 524288 | tf_op jit(solution)/shard_map/psum | solution.py:94
  107.5 130.2 %copy-start.2 = (bf16[256,128]{1,0:T(8,128)(2,1)S(1)}, bf16[256,128]{1,0:T(8,128)(2,1)}, u32[]{:S(2)}) copy-start(bf16[256,128]{1,0:T(8,128)(2,1)} %param.7) | copy-start | bytes 196612
Sparse Core Ops, SparseCore 0:
  109.8 127.8 all-reduce.1
where the time goes:
time: 298 us; the launch traced here: 296 us
  waiting for transfers between devices  128 us (43%)
  other arithmetic  67.7 us (23%)
  between operations  54.4 us (18%)
  matrix products  31.8 us (11%)
  starting transfers between devices  7.54 us (3%)
  local copies, waits for them, and re-layouts  6.83 us (2%)
    psum x1, waiting for transfers between devices, shards(): data_gram = lax.psum(local_gram, ('wide', 'narrow'))  128 us
    add x2, other arithmetic, band_matrix(): matrix + jnp.where(offset_index == offset, weights[offset], jnp.float32(0...  19.2 us
    another operation x3, other arithmetic, shards(): jnp.linalg.cholesky(high_dot(projected.T, high_dot(data_gram, projected)))  12.6 us
    another operation x3, other arithmetic, shards(): first_lower = jnp.linalg.cholesky(high_dot(sketch_full.T, weighted))  12.4 us
    dot_general x1, matrix products, filter_volumes(): jnp.einsum('or,...rc->...oc', band_matrix(3.0, row_count), column_pass[.....  11.5 us
    dot_general x1, matrix products, filter_volumes(): jnp.einsum('or,...rc->...oc', band_matrix(1.5, row_count), column_pass[.....  11.4 us
    another operation x2, other arithmetic, shards(): jax.scipy.linalg.solve_triangular(first_lower, weighted.T, lower=True)  10.5 us
    another operation x1, other arithmetic, shards(): jax.scipy.linalg.solve_triangular(second_lower, projected.T, lower=True)  9.81 us
  transfers between devices with their start and end apart: 2, of which 1 were waited for; matrix products, arithmetic and copies ran while one was open for 1% of the time, Pallas kernels for 0%

commit v1 on v0

--- a/solution.py
+++ b/solution.py
@@ -76,7 +76,15 @@
     length = per_device * group_size
     toeplitz = build_toeplitz(kernel_taps, length)
     arranged = flattened.reshape(1, per_device, group_size, block)
-    received = lax.all_to_all(arranged, ("wide", "narrow"), split_axis=2, concat_axis=0, tiled=True)
+    received = jnp.concatenate(
+        lax.all_to_all(
+            jnp.stack(jnp.split(arranged, lax.axis_size(("wide", "narrow")), axis=2)),
+            ("wide", "narrow"),
+            0,
+            0,
+        ),
+        axis=0,
+    )
     deconvolved = jnp.dot(
         toeplitz, received.reshape(length, received.shape[3]), preferred_element_type=jnp.float32
     ).astype(jnp.bfloat16)

time: 298 us -> 317 us (1.064)
  local copies, waits for them, and re-layouts: 6.83 us -> 26.5 us
    unnamed x7 -> x38, local copies, waits for them, and re-layouts: 0.75 us -> 19.7 us
where the time goes in v1:
time: 317 us; the launch traced here: 316 us
  waiting for transfers between devices  128 us (40%)
  other arithmetic  67.7 us (21%)
  between operations  54.5 us (17%)
  matrix products  31.8 us (10%)
  local copies, waits for them, and re-layouts  26.5 us (8%)
  starting transfers between devices  7.54 us (2%)
    psum x1, waiting for transfers between devices, shards(): data_gram = lax.psum(local_gram, ('wide', 'narrow'))  128 us
    unnamed x38, local copies, waits for them, and re-layouts  19.7 us
    add x2, other arithmetic, band_matrix(): matrix + jnp.where(offset_index == offset, weights[offset], jnp.float32(0...  19.2 us
    another operation x3, other arithmetic, shards(): jnp.linalg.cholesky(high_dot(projected.T, high_dot(data_gram, projected)))  12.6 us
    another operation x3, other arithmetic, shards(): first_lower = jnp.linalg.cholesky(high_dot(sketch_full.T, weighted))  12.4 us
    dot_general x1, matrix products, filter_volumes(): jnp.einsum('or,...rc->...oc', band_matrix(3.0, row_count), column_pass[.....  11.5 us
    dot_general x1, matrix products, filter_volumes(): jnp.einsum('or,...rc->...oc', band_matrix(1.5, row_count), column_pass[.....  11.4 us
    another operation x2, other arithmetic, shards(): jax.scipy.linalg.solve_triangular(first_lower, weighted.T, lower=True)  10.5 us
  transfers between devices with their start and end apart: 2, of which 1 were waited for; matrix products, arithmetic and copies ran while one was open for 1% of the time, Pallas kernels for 0%

profile of v1, /device:TPU:0, one launch (start us, length us, event | category | flops | bytes accessed | tf_op | source)
XLA Modules:
  0.0 316.0 jit_solution(10308475412119456054)
XLA Ops:
  7.2 0.6 fusion.237
  7.8 0.6 fusion.238
  8.4 0.7 broadcast_divide_fusion.1
  9.1 0.7 fusion.343
  9.8 0.7 broadcast_divide_fusion
  10.4 0.7 fusion.344
  11.1 9.6 %select_add_fusion.1 = f32[128,256]{1,0:T(8,128)S(1)} fusion(f32[]{:T(128)} %bitcast.78, f32[]{:T(128)} %bitcast.77, f32[]{:T(128)} %bitcast.76, f32[]{:T(128)} %bitcast.75, f32[]{:T(128)} %bitcast.74, f32[]{:T(128)} %bitcast.73, f32[]{:T(128)} %bitcast.72, f32[]{:T(128)} %bitcast.71, f32[]{:T(128)} %bitcast.70, f32[]{:T(128)} %bitcast.69, f32[]{:T(128)} %bitcast.68, ...), kind=kLoop, calls=%fused_computation.85 | loop fusion | flops 1507328 | bytes 131644 | tf_op jit(solution)/shard_map/add | solution.py:23
  20.7 9.7 %select_add_fusion = f32[128,256]{1,0:T(8,128)S(1)} fusion(f32[]{:T(128)} %bitcast.93, f32[]{:T(128)} %bitcast.92, f32[]{:T(128)} %bitcast.91, f32[]{:T(128)} %bitcast.90, f32[]{:T(128)} %bitcast.89, f32[]{:T(128)} %bitcast.88, f32[]{:T(128)} %bitcast.87, f32[]{:T(128)} %bitcast.86, f32[]{:T(128)} %bitcast.85, f32[]{:T(128)} %bitcast.84, f32[]{:T(128)} %bitcast.83, ...), kind=kLoop, calls=%fused_computation.84 | loop fusion | flops 1507328 | bytes 131644 | tf_op jit(solution)/shard_map/add | solution.py:23
  30.4 1.9 convolution_bitcast_fusion
  32.3 11.5 %fusion = f32[8,2,128,128]{3,2,1,0:T(8,128)S(1)} fusion(f32[8,2,256,256]{2,3,1,0:T(8,128)S(1)} %convolution_bitcast_fusion, f32[]{:T(128)} %bitcast.93, f32[]{:T(128)} %bitcast.92, f32[]{:T(128)} %bitcast.91, f32[]{:T(128)} %bitcast.90, f32[]{:T(128)} %bitcast.89, f32[]{:T(128)} %bitcast.88, f32[]{:T(128)} %bitcast.87, f32[]{:T(128)} %bitcast.86, ...), kind=kOutput, calls=%fused_computation.1 | convolution fusion | flops 806813696 | bytes 3146300 | tf_op jit(solution)/shard_map/or,...rc->...oc/dot_general | solution.py:44
  43.8 11.4 %fusion.10 = bf16[8,2,128,128]{2,3,1,0:T(8,128)(2,1)S(1)} fusion(f32[8,2,128,128]{3,2,1,0:T(8,128)S(1)} %fusion, f32[8,2,256,256]{2,3,1,0:T(8,128)S(1)} %convolution_bitcast_fusion, f32[]{:T(128)} %bitcast.78, f32[]{:T(128)} %bitcast.77, f32[]{:T(128)} %bitcast.76, f32[]{:T(128)} %bitcast.75, f32[]{:T(128)} %bitcast.74, f32[]{:T(128)} %bitcast.73, ...), kind=kOutput, calls=%fused_computation.8 | convolution fusion | flops 807337984 | bytes 3670588 | tf_op jit(solution)/shard_map/or,...rc->...oc/dot_general | solution.py:38
  56.2 0.7 fusion.337
  56.9 0.6 constant_dynamic-update-slice_fusion.31
  59.3 0.6 constant_dynamic-update-slice_fusion.27
  60.0 0.6 constant_dynamic-update-slice_fusion.26
  60.6 0.6 constant_dynamic-update-slice_fusion.25
  61.2 0.6 constant_dynamic-update-slice_fusion.24
  61.8 0.6 constant_dynamic-update-slice_fusion.23
  64.9 0.6 constant_dynamic-update-slice_fusion.18
  65.5 0.6 constant_dynamic-update-slice_fusion.17
  66.1 0.6 constant_dynamic-update-slice_fusion.16
  66.7 0.6 constant_dynamic-update-slice_fusion.15
  67.3 0.6 constant_dynamic-update-slice_fusion.14
  67.9 0.6 constant_dynamic-update-slice_fusion.13
  71.0 0.6 constant_dynamic-update-slice_fusion.8
  71.6 0.6 constant_dynamic-update-slice_fusion.7
  72.2 0.6 constant_dynamic-update-slice_fusion.6
  72.8 0.6 constant_dynamic-update-slice_fusion.5
  76.5 7.3 %all-to-all-start = ((bf16[32,1,8,1,1024]{4,2,3,1,0:T(8,128)(2,1)}), bf16[32,1,8,1,1024]{4,2,3,1,0:T(8,128)(2,1)S(1)}, u32[]{:S(2)}, u32[]{:S(2)}) async-start(bf16[32,1,8,1,1024]{4,2,3,1,0:T(8,128)(2,1)} %constant_dynamic-update-slice_fusion), calls=%async_computation | async-start | bytes 1048576 | tf_op jit(solution)/shard_map/all_to_all | solution.py:80
  84.1 0.7 fusion.340
  89.8 0.7 fusion.339
  103.2 0.7 fusion.341
  122.1 0.7 fusion.342
  127.2 1.1 convolution_convert_fusion
  128.3 1.0 convolution_multiply_fusion
  129.3 128.0 %all-reduce.2.cloned.1.call-done = f32[256,256]{1,0:T(8,128)} async-done(((f32[256,256]{1,0:T(8,128)}), f32[256,256]{1,0:T(8,128)}) %all-reduce.2.cloned.1.call-update) | async-done | bytes 262160 | tf_op jit(solution)/shard_map/psum | solution.py:102
  257.4 1.2 fusion.345
  259.0 11.7 %cholesky.44 = f32[128,128]{1,0:T(8,128)S(1)} custom-call(f32[128,128]{1,0:T(8,128)S(1)} %add_multiply_fusion), custom_call_target="Cholesky" | custom-call | tf_op jit(solution)/shard_map/jit(cholesky)/cholesky | solution.py:105
  270.7 0.6 compare_reduce_fusion.1
  271.4 0.7 fusion.228
  272.0 9.8 %custom-call.6 = f32[1,128,128]{1,2,0:T(8,128)S(1)} custom-call(f32[1,128,128]{2,1,0:T(8,128)S(1)} %fusion.228), custom_call_target="InvertDiagBlocksLowerTriangular" | custom-call | tf_op jit(solution)/shard_map/jit(_solve_triangular)/triangular_solve | solution.py:106
  282.2 1.3 fusion.347
  283.9 11.9 %cholesky.55 = f32[128,128]{1,0:T(8,128)S(1)} custom-call(f32[128,128]{1,0:T(8,128)S(1)} %fusion.231), custom_call_target="Cholesky" | custom-call | tf_op jit(solution)/shard_map/jit(cholesky)/cholesky | solution.py:107
  295.8 0.6 compare_reduce_fusion
  296.5 0.7 fusion.236
  297.1 9.8 %custom-call.7 = f32[1,128,128]{1,2,0:T(8,128)S(1)} custom-call(f32[1,128,128]{2,1,0:T(8,128)S(1)} %get-tuple-element.101), custom_call_target="InvertDiagBlocksLowerTriangular" | custom-call | tf_op jit(solution)/shard_map/jit(_solve_triangular)/triangular_solve | solution.py:108
  307.2 1.2 fusion.349
  308.4 0.7 copy.627
  (39 shorter events, 12.5 us)
Async XLA Ops:
  7.2 23.2 %copy-start = (bf16[8,2,256,256]{3,2,1,0:T(8,128)(2,1)S(1)}, bf16[8,2,256,256]{3,2,1,0:T(8,128)(2,1)}, u32[]{:S(2)}) copy-start(bf16[8,2,256,256]{3,2,1,0:T(8,128)(2,1)} %param.6) | copy-start | bytes 6291460
  56.2 27.9 %copy-start.1 = (bf16[64]{0:T(256)(128)(2,1)S(1)}, bf16[64]{0:T(256)(128)(2,1)}, u32[]{:S(2)}) copy-start(bf16[64]{0:T(256)(128)(2,1)} %param.8) | copy-start | bytes 388
  76.5 50.7 %all-to-all-start = ((bf16[32,1,8,1,1024]{4,2,3,1,0:T(8,128)(2,1)}), bf16[32,1,8,1,1024]{4,2,3,1,0:T(8,128)(2,1)S(1)}, u32[]{:S(2)}, u32[]{:S(2)}) async-start(bf16[32,1,8,1,1024]{4,2,3,1,0:T(8,128)(2,1)} %constant_dynamic-update-slice_fusion), calls=%async_computation | async-start | bytes 1048576 | tf_op jit(solution)/shard_map/all_to_all | solution.py:80
  83.8 173.5 %all-reduce.2.cloned.1.call-start = ((), (), s32[]{:S(2)}) async-start(), calls=%async_computation.1 | async-start | bytes 524288 | tf_op jit(solution)/shard_map/psum | solution.py:102
  127.2 130.2 %copy-start.2 = (bf16[256,128]{1,0:T(8,128)(2,1)S(1)}, bf16[256,128]{1,0:T(8,128)(2,1)}, u32[]{:S(2)}) copy-start(bf16[256,128]{1,0:T(8,128)(2,1)} %param.7) | copy-start | bytes 196612
Sparse Core Ops, SparseCore 0:
  129.5 127.8 all-reduce.1
